TPU v7x, 32 devices: a whole 2x2x4 slice. The times are simulated.
32 devices in a mesh: shard: 2 (over y), ctx: 4 (over z), tp: 4 (over x, core).
Axes of the slice: x: 2, y: 2, z: 4, core: 2. Of those that a mesh axis runs over, the one named last changes fastest.
Arguments:
- inputs: bfloat16 [2, 4096, 768], P('shard', 'ctx'), may hold values from -6 to 6
- lengths: int32 [2], P('shard'), may hold values from 1024 to 4096, as said below
- global_blocks: int32 [2, 2], P('shard'), may hold values from 0 to 15, as said below
- random_blocks: int32 [2, 64, 3], P('shard', 'ctx'), may hold values from 0 to 63
- master_blocks: float32 [768, 96, 96], P(('shard', 'ctx', 'tp'))
- outer_vectors: float32 [6, 768], replicated
- inner_biases: float32 [4, 1152], P('tp'), may hold values from -4 to 4
- left_stats: float32 [768, 96, 96], P(('shard', 'ctx', 'tp')), as said below
- right_stats: float32 [768, 96, 96], P(('shard', 'ctx', 'tp')), as said below
- left_roots: float32 [768, 96, 96], P(('shard', 'ctx', 'tp')), as said below
- right_roots: float32 [768, 96, 96], P(('shard', 'ctx', 'tp')), as said below
- cotangent: bfloat16 [2, 4096, 768], P('shard', 'ctx'), may hold values from -6 to 6
Outputs:
- output: bfloat16 [2, 4096, 768], P('shard', 'ctx')
- input_grad: bfloat16 [2, 4096, 768], P('shard', 'ctx')
- block_grads: float32 [768, 96, 96], P(('shard', 'ctx', 'tp'))
- outer_grads: float32 [6, 768], P(None, ('shard', 'ctx'))
- inner_grads: float32 [4, 1152], P('tp', ('shard', 'ctx'))
- maxima: float32 [12], P('tp')
- left_new: float32 [768, 96, 96], P(('shard', 'ctx', 'tp'))
- right_new: float32 [768, 96, 96], P(('shard', 'ctx', 'tp'))
- new_blocks: float32 [768, 96, 96], P(('shard', 'ctx', 'tp'))
- new_outer: float32 [6, 768], P(None, ('shard', 'ctx'))
- new_inner: float32 [4, 1152], P('tp', ('shard', 'ctx'))
Inputs may be any that keep to these rules, and one draw needn't show every extreme that they name: `lengths`: sequence 0 holds 4096 valid tokens. `global_blocks`: the two ids of a sequence differ. `left_stats`: each block is symmetric. `right_stats`: each block is symmetric. `left_roots`: each block is symmetric. `right_roots`: each block is symmetric.
All inputs are finite; a program needn't handle non-finite values.
Results may differ from a plain program's by a relative error of at most 0.018.
Values may be sent and summed in bfloat16 or wider, within the bound.
No kernel may reach another device: no remote copies, remote signals or barrier semaphores. Data moves between devices by JAX's collectives and lax.ppermute only.
A program may use at most 192 MiB of HBM per device.

v0:
```python
import jax
import jax.numpy as jnp
from jax import lax
from jax.sharding import PartitionSpec as P

D = 768
HEADS = 12
HEAD = 64
FF = 3072
BLOCK = 64
SEQ = 4096
PB = 96
eps_norm = 1e-06
tau_clip = 9.0
rate_matrix = 0.3
rate_vector = 0.001
neg_large = -1e30
high = lax.Precision.HIGHEST


def layer_norm(values, gain, shift):
    mean_val = jnp.mean(values, axis=-1, keepdims=True)
    centred = values - mean_val
    var_val = jnp.mean(centred * centred, axis=-1, keepdims=True)
    return centred * lax.rsqrt(var_val + eps_norm) * gain + shift


def gelu_tanh(values):
    return jax.nn.gelu(values, approximate=True)


def to_grid(blocks, row_count, col_count):
    shaped = blocks.reshape(row_count // PB, col_count // PB, PB, PB)
    return shaped.transpose(0, 2, 1, 3).reshape(row_count, col_count)


def from_grid(matrix):
    row_count, col_count = matrix.shape
    shaped = matrix.reshape(row_count // PB, PB, col_count // PB, PB)
    return shaped.transpose(0, 2, 1, 3).reshape(-1, PB, PB)


def unpack_weights(whole, head_cols, unit_count):
    first_end = D // PB * (3 * head_cols // PB)
    second_end = first_end + head_cols // PB * (D // PB)
    third_end = second_end + D // PB * (unit_count // PB)
    return (
        to_grid(whole[:first_end], D, 3 * head_cols),
        to_grid(whole[first_end:second_end], head_cols, D),
        to_grid(whole[second_end:third_end], D, unit_count),
        to_grid(whole[third_end:], unit_count, D),
    )


def block_layout(slot_length, global_ids, random_ids, first_block, rows_blocks, block_count):
    rows = first_block + jnp.arange(rows_blocks, dtype=jnp.int32)
    window = jnp.stack([rows - 1, rows, rows + 1], axis=1)
    globals_row = jnp.broadcast_to(global_ids[None, :], (rows_blocks, 2))
    listed = jnp.concatenate([window, globals_row, random_ids], axis=1)
    inside = (listed >= 0) & (listed < block_count)
    clipped = jnp.clip(listed, 0, block_count - 1)
    key_pos = listed[:, :, None] * BLOCK + jnp.arange(BLOCK, dtype=jnp.int32)[None, None, :]
    key_mask = (inside[:, :, None] & (key_pos < slot_length)).reshape(rows_blocks, -1)
    query_pos = (first_block * BLOCK + jnp.arange(rows_blocks * BLOCK, dtype=jnp.int32)).reshape(
        rows_blocks, BLOCK
    )
    return (clipped, key_mask, query_pos < slot_length)


def pick_blocks(full_rows, clipped, head_count):
    block_count = full_rows.shape[0] // BLOCK
    picked = full_rows.reshape(block_count, BLOCK, -1)[clipped]
    return picked.reshape(clipped.shape[0], clipped.shape[1] * BLOCK, head_count, HEAD)


def attend_scores(query_blocks, key_blocks):
    return jnp.einsum(
        "lqhd,lkhd->lhqk", query_blocks, key_blocks, preferred_element_type=jnp.float32
    ) * HEAD ** (-0.5)


def probs_again(query_blocks, d_out_blocks, key_blocks, value_blocks, key_mask, lse_blk):
    raw_scores = attend_scores(query_blocks, key_blocks)
    probs = jnp.exp(jnp.where(key_mask[:, None, None, :], raw_scores, neg_large) - lse_blk)
    d_probs = jnp.einsum(
        "lqhd,lkhd->lhqk", d_out_blocks, value_blocks, preferred_element_type=jnp.float32
    )
    return (probs, d_probs)


def group_back(
    query_blocks,
    d_out_blocks,
    key_src,
    value_src,
    clipped,
    key_mask,
    lse_blk,
    delta_blk,
    block_count,
):
    rows_blocks, _, heads_here, _ = query_blocks.shape
    head_cols = heads_here * HEAD
    key_blocks = pick_blocks(key_src, clipped, heads_here)
    value_blocks = pick_blocks(value_src, clipped, heads_here)
    probs, d_probs = probs_again(
        query_blocks, d_out_blocks, key_blocks, value_blocks, key_mask, lse_blk
    )
    delta_blk = jnp.sum(probs * d_probs, axis=-1, keepdims=True)
    d_scores = (probs * (d_probs - delta_blk)).astype(jnp.bfloat16)
    d_query = jnp.einsum(
        "lhqk,lkhd->lqhd", d_scores, key_blocks, preferred_element_type=jnp.float32
    ) * HEAD ** (-0.5)
    d_key_blocks = jnp.einsum(
        "lhqk,lqhd->lkhd", d_scores, query_blocks, preferred_element_type=jnp.float32
    ) * HEAD ** (-0.5)
    d_value_blocks = jnp.einsum(
        "lhqk,lqhd->lkhd",
        probs.astype(jnp.bfloat16),
        d_out_blocks,
        preferred_element_type=jnp.float32,
    )
    listed_count = clipped.shape[1]
    d_key_full = (
        jnp.zeros((block_count, BLOCK, head_cols), jnp.float32)
        .at[clipped]
        .add(d_key_blocks.reshape(rows_blocks, listed_count, BLOCK, head_cols))
    )
    d_value_full = (
        jnp.zeros((block_count, BLOCK, head_cols), jnp.float32)
        .at[clipped]
        .add(d_value_blocks.reshape(rows_blocks, listed_count, BLOCK, head_cols))
    )
    return (
        d_query.reshape(-1, head_cols),
        d_key_full.reshape(-1, head_cols),
        d_value_full.reshape(-1, head_cols),
    )


def per_device(
    inputs,
    lengths,
    global_blocks,
    random_blocks,
    master_blocks,
    outer_vectors,
    inner_biases,
    left_stats,
    right_stats,
    left_roots,
    right_roots,
    cotangent,
):
    tensor_count = lax.axis_size("tp")
    owner_count = lax.axis_size(("shard", "ctx"))
    heads_here = HEADS // tensor_count
    head_cols = heads_here * HEAD
    unit_count = FF // tensor_count
    slot_count, ctx_tokens, _ = inputs.shape
    rows_blocks = ctx_tokens // BLOCK
    block_count = SEQ // BLOCK
    ctx_index = lax.axis_index("ctx")
    owner_index = lax.axis_index(("shard", "ctx"))
    gathered = lax.all_gather(
        master_blocks.astype(jnp.bfloat16), ("shard", "ctx"), axis=0, tiled=True
    )
    w_qkv, w_out, w_up, w_down = unpack_weights(gathered, head_cols, unit_count)
    flat_in = inputs.reshape(-1, D)
    inner_row = inner_biases[0]
    q_bias = inner_row[:head_cols]
    v_bias = inner_row[head_cols : 2 * head_cols]
    up_bias = inner_row[2 * head_cols :]
    projected = jnp.dot(flat_in, w_qkv, preferred_element_type=jnp.float32)
    queries = (projected[:, :head_cols] + q_bias).astype(jnp.bfloat16)
    key_rows = (
        projected[:, head_cols : 2 * head_cols]
        .astype(jnp.bfloat16)
        .reshape(slot_count, ctx_tokens, head_cols)
    )
    value_rows = (
        (projected[:, 2 * head_cols :] + v_bias)
        .astype(jnp.bfloat16)
        .reshape(slot_count, ctx_tokens, head_cols)
    )
    keys_all, values_all = (
        lax.all_gather(key_rows, "ctx", axis=1, tiled=True),
        lax.all_gather(value_rows, "ctx", axis=1, tiled=True),
    )
    query_slots = queries.reshape(slot_count, ctx_tokens, head_cols)
    peak_logit = jnp.full((heads_here,), neg_large, jnp.float32)
    slot_index = 0
    clipped, key_mask, query_mask = block_layout(
        lengths[slot_index],
        global_blocks[slot_index],
        random_blocks[slot_index],
        ctx_index * rows_blocks,
        rows_blocks,
        block_count,
    )
    layouts = [(clipped, key_mask)]
    query_blocks = query_slots[slot_index].reshape(rows_blocks, BLOCK, heads_here, HEAD)
    key_blocks = pick_blocks(keys_all[slot_index], clipped, heads_here)
    value_blocks = pick_blocks(values_all[slot_index], clipped, heads_here)
    raw_scores = attend_scores(query_blocks, key_blocks)
    both_mask = key_mask[:, None, None, :] & query_mask[:, None, :, None]
    peak_logit = jnp.maximum(
        peak_logit, jnp.max(jnp.where(both_mask, raw_scores, neg_large), axis=(0, 2, 3))
    )
    masked = jnp.where(key_mask[:, None, None, :], raw_scores, neg_large)
    row_top = jnp.max(masked, axis=-1, keepdims=True)
    shifted = jnp.exp(masked - row_top)
    row_total = jnp.sum(shifted, axis=-1, keepdims=True)
    probs = shifted / row_total
    lse_list = [row_top + jnp.log(row_total)]
    attended = jnp.einsum(
        "lhqk,lkhd->lqhd",
        probs.astype(jnp.bfloat16),
        value_blocks,
        preferred_element_type=jnp.float32,
    )
    attended_list = attended.reshape(ctx_tokens, head_cols)
    attended_low = attended_list.astype(jnp.bfloat16)
    branch = (
        lax.psum(jnp.dot(attended_low, w_out, preferred_element_type=jnp.float32), "tp")
        + outer_vectors[0]
    )
    hidden_in = flat_in.astype(jnp.float32) + branch
    x_first = layer_norm(hidden_in, outer_vectors[2], outer_vectors[3])
    x_first_low = x_first.astype(jnp.bfloat16)
    gate_pre = jnp.dot(x_first_low, w_up, preferred_element_type=jnp.float32) + up_bias
    act_low = gelu_tanh(gate_pre).astype(jnp.bfloat16)
    ff_out = (
        lax.psum(jnp.dot(act_low, w_down, preferred_element_type=jnp.float32), "tp")
        + outer_vectors[1]
    )
    mixed_sum = x_first + ff_out
    result = layer_norm(mixed_sum, outer_vectors[4], outer_vectors[5])
    maxima = lax.pmax(peak_logit, ("shard", "ctx"))
    positions = ctx_index * ctx_tokens + jnp.arange(ctx_tokens, dtype=jnp.int32)
    row_valid = (positions[None, :] < lengths[:, None]).astype(jnp.float32).reshape(-1)
    d_result = cotangent.reshape(-1, D).astype(jnp.float32) * row_valid[:, None]
    regathered = lax.all_gather(
        master_blocks.astype(jnp.bfloat16), ("shard", "ctx"), axis=0, tiled=True
    )
    wb_qkv, wb_out, wb_up, wb_down = unpack_weights(regathered, head_cols, unit_count)
    _, back_second = jax.vjp(layer_norm, mixed_sum, outer_vectors[4], outer_vectors[5])
    d_mixed, d_gain2, d_shift2 = back_second(d_result)
    d_ff_low = d_mixed.astype(jnp.bfloat16)
    d_bias2 = jnp.sum(d_ff_low.astype(jnp.float32), axis=0)
    g_down = jnp.dot(act_low.T, d_ff_low, preferred_element_type=jnp.float32)
    d_act = jnp.dot(d_ff_low, wb_down.T, preferred_element_type=jnp.float32)
    _, back_gelu = jax.vjp(gelu_tanh, gate_pre)
    d_gate_low = back_gelu(d_act)[0].astype(jnp.bfloat16)
    d_upbias = jnp.sum(d_gate_low.astype(jnp.float32), axis=0)
    g_up = jnp.dot(x_first_low.T, d_gate_low, preferred_element_type=jnp.float32)
    d_first = d_mixed + lax.psum(
        jnp.dot(d_gate_low, wb_up.T, preferred_element_type=jnp.float32), "tp"
    )
    _, back_first = jax.vjp(layer_norm, hidden_in, outer_vectors[2], outer_vectors[3])
    d_hidden, d_gain1, d_shift1 = back_first(d_first)
    d_branch_low = d_hidden.astype(jnp.bfloat16)
    d_bias_out = jnp.sum(d_branch_low.astype(jnp.float32), axis=0)
    g_out = jnp.dot(attended_low.T, d_branch_low, preferred_element_type=jnp.float32)
    d_att_low = jnp.dot(d_branch_low, wb_out.T, preferred_element_type=jnp.float32).astype(
        jnp.bfloat16
    )
    d_att_slots = d_att_low.reshape(slot_count, ctx_tokens, head_cols)
    keys_back, values_back = (keys_all, values_all)
    slot_index = 0
    clipped, key_mask = layouts[slot_index]
    query_blocks = query_slots[slot_index].reshape(rows_blocks, BLOCK, heads_here, HEAD)
    d_out_blocks = d_att_slots[slot_index].reshape(rows_blocks, BLOCK, heads_here, HEAD)
    d_query, d_key_full, d_value_full = group_back(
        query_blocks,
        d_out_blocks,
        keys_back[slot_index],
        values_back[slot_index],
        clipped,
        key_mask,
        lse_list[slot_index],
        None,
        block_count,
    )
    dk_list = [d_key_full]
    dv_list = [d_value_full]
    d_keys, d_values = (
        lax.psum_scatter(
            jnp.stack(dk_list).astype(jnp.bfloat16), "ctx", scatter_dimension=1, tiled=True
        ).astype(jnp.float32),
        lax.psum_scatter(
            jnp.stack(dv_list).astype(jnp.bfloat16), "ctx", scatter_dimension=1, tiled=True
        ).astype(jnp.float32),
    )
    d_q_low = d_query.astype(jnp.bfloat16)
    d_k_low = d_keys.reshape(-1, head_cols).astype(jnp.bfloat16)
    d_v_low = d_values.reshape(-1, head_cols).astype(jnp.bfloat16)
    d_proj = jnp.concatenate([d_q_low, d_k_low, d_v_low], axis=1)
    d_qbias = jnp.sum(d_q_low.astype(jnp.float32), axis=0)
    d_vbias = jnp.sum(d_v_low.astype(jnp.float32), axis=0)
    g_qkv = jnp.dot(flat_in.T, d_proj, preferred_element_type=jnp.float32)
    d_inputs = d_hidden + lax.psum(
        jnp.dot(d_proj, wb_qkv.T, preferred_element_type=jnp.float32).astype(jnp.bfloat16), "tp"
    ).astype(jnp.float32)
    input_grad = d_inputs.reshape(inputs.shape).astype(jnp.bfloat16)
    blocks_grad = jnp.concatenate(
        [from_grid(g_qkv), from_grid(g_out), from_grid(g_up), from_grid(g_down)], axis=0
    )
    outer_part = jnp.stack([d_bias_out, d_bias2, d_gain1, d_shift1, d_gain2, d_shift2], axis=0)
    inner_part = jnp.concatenate([d_qbias, d_vbias, d_upbias])[None, :]
    block_sum, outer_sum, inner_sum = (
        lax.psum_scatter(blocks_grad, ("shard", "ctx"), scatter_dimension=0, tiled=True),
        lax.psum_scatter(outer_part, ("shard", "ctx"), scatter_dimension=1, tiled=True),
        lax.psum_scatter(inner_part, ("shard", "ctx"), scatter_dimension=1, tiled=True),
    )
    left_new = 0.5 * left_stats + 0.5 * jnp.einsum(
        "bij,bkj->bik", block_sum, block_sum, precision=high
    )
    right_new = 0.5 * right_stats + 0.5 * jnp.einsum(
        "bji,bjk->bik", block_sum, block_sum, precision=high
    )
    left_applied = jnp.einsum("bij,bjk->bik", left_roots, block_sum, precision=high)
    step_val = jnp.einsum("bij,bjk->bik", left_applied, right_roots, precision=high)
    clip_sqrt = jnp.sqrt(tau_clip / jnp.maximum(maxima, tau_clip))
    head_factor = jnp.repeat(clip_sqrt, HEAD)
    table = jnp.concatenate([head_factor, head_factor, jnp.ones((head_cols,), jnp.float32)])
    qkv_factor = jnp.tile(table.reshape(1, -1, PB), (D // PB, 1, 1)).reshape(-1, PB)
    blocks_here = master_blocks.shape[0]
    all_factor = jnp.concatenate(
        [qkv_factor, jnp.ones((blocks_here * owner_count - qkv_factor.shape[0], PB), jnp.float32)],
        axis=0,
    )
    own_factor = lax.dynamic_slice_in_dim(all_factor, owner_index * blocks_here, blocks_here, 0)
    new_blocks = (master_blocks - rate_matrix * step_val) * own_factor[:, None, :]
    outer_cols = D // owner_count
    own_outer = lax.dynamic_slice_in_dim(outer_vectors, owner_index * outer_cols, outer_cols, 1)
    new_outer = own_outer - rate_vector * outer_sum
    inner_cols = inner_biases.shape[1] // owner_count
    inner_factor = jnp.concatenate([head_factor, jnp.ones((head_cols + unit_count,), jnp.float32)])
    own_inner_factor = lax.dynamic_slice_in_dim(
        inner_factor, owner_index * inner_cols, inner_cols, 0
    )
    own_inner = lax.dynamic_slice_in_dim(inner_biases, owner_index * inner_cols, inner_cols, 1)
    new_inner = (own_inner - rate_vector * inner_sum) * own_inner_factor[None, :]
    output = result.reshape(inputs.shape).astype(jnp.bfloat16)
    return (
        output,
        input_grad,
        block_sum,
        outer_sum,
        inner_sum,
        maxima,
        left_new,
        right_new,
        new_blocks,
        new_outer,
        new_inner,
    )


def solution(mesh):
    return jax.shard_map(
        per_device,
        mesh=mesh,
        in_specs=(
            P("shard", "ctx", None),
            P("shard"),
            P("shard", None),
            P("shard", "ctx", None),
            P(("shard", "ctx", "tp"), None, None),
            P(),
            P("tp", None),
            P(("shard", "ctx", "tp"), None, None),
            P(("shard", "ctx", "tp"), None, None),
            P(("shard", "ctx", "tp"), None, None),
            P(("shard", "ctx", "tp"), None, None),
            P("shard", "ctx", None),
        ),
        out_specs=(
            P("shard", "ctx", None),
            P("shard", "ctx", None),
            P(("shard", "ctx", "tp"), None, None),
            P(None, ("shard", "ctx")),
            P("tp", ("shard", "ctx")),
            P("tp"),
            P(("shard", "ctx", "tp"), None, None),
            P(("shard", "ctx", "tp"), None, None),
            P(("shard", "ctx", "tp"), None, None),
            P(None, ("shard", "ctx")),
            P("tp", ("shard", "ctx")),
        ),
        check_vma=False,
    )
```

profile of v0, /device:TPU:0, one launch (start us, length us, event | category | flops | bytes accessed | tf_op | source)
XLA Modules:
  0.0 1027.7 jit_solution(3224889106006550222)
XLA Ops:
  9.6 83.2 %all-gather.6.cloned.1.call-done = bf16[192,96,96]{2,1,0:T(8,128)(2,1)} async-done(((bf16[24,96,96]{2,1,0:T(8,128)(2,1)}), bf16[192,96,96]{2,1,0:T(8,128)(2,1)}) %all-gather.6.cloned.1.call-update) | async-done | bytes 3538960 | tf_op jit(solution)/shard_map/all_gather | solution.py:165
  109.1 27.4 %all-gather.10.cloned.1.call-done = bf16[4096,192]{0,1:T(8,128)(2,1)} async-done(((bf16[1024,192]{0,1:T(8,128)(2,1)}), bf16[4096,192]{0,1:T(8,128)(2,1)}) %all-gather.10.cloned.1.call-update) | async-done | bytes 1572880 | tf_op jit(solution)/shard_map/all_gather | solution.py:187
  142.4 15.9 %reshape.559 = bf16[16,512,3,64]{3,2,1,0:T(4,128)(2,1)} reshape(bf16[128,64,192]{2,1,0:T(8,128)(2,1)} %gather_fusion.1) | data formatting | bytes 6291456 | tf_op jit(solution)/shard_map/reshape | solution.py:73
  158.4 12.2 %copy.106 = bf16[16,512,3,64]{1,3,2,0:T(8,128)(2,1)} copy(bf16[16,512,3,64]{3,2,1,0:T(4,128)(2,1)} %reshape.559) | data formatting | bytes 6291456 | tf_op jit(solution)/shard_map/reshape | solution.py:73
  180.5 15.9 %reshape.558 = bf16[16,512,3,64]{3,2,1,0:T(4,128)(2,1)} reshape(bf16[128,64,192]{2,1,0:T(8,128)(2,1)} %gather_fusion) | data formatting | bytes 6291456 | tf_op jit(solution)/shard_map/reshape | solution.py:73
  196.4 12.3 %copy.107 = bf16[16,512,3,64]{1,3,2,0:T(8,128)(2,1)} copy(bf16[16,512,3,64]{3,2,1,0:T(4,128)(2,1)} %reshape.558) | data formatting | bytes 6291456 | tf_op jit(solution)/shard_map/reshape | solution.py:73
  237.2 52.6 %all-reduce.7.cloned.1.call-done = f32[1024,768]{1,0:T(8,128)} async-done(((f32[1024,768]{1,0:T(8,128)}), f32[1024,768]{1,0:T(8,128)}) %all-reduce.7.cloned.1.call-update) | async-done | bytes 3145744 | tf_op jit(solution)/shard_map/psum | solution.py:225
  302.4 67.8 %all-reduce.9.cloned.1.call-done = f32[1024,768]{1,0:T(8,128)} async-done(((f32[1024,768]{1,0:T(8,128)}), f32[1024,768]{1,0:T(8,128)}) %all-reduce.9.cloned.1.call-update) | async-done | bytes 3145744 | tf_op jit(solution)/shard_map/psum | solution.py:234
  393.6 67.9 %all-reduce.11.cloned.1.call-done = f32[1024,768]{1,0:T(8,128)} async-done(((f32[1024,768]{1,0:T(8,128)}), f32[1024,768]{1,0:T(8,128)}) %all-reduce.11.cloned.1.call-update) | async-done | bytes 3145744 | tf_op jit(solution)/shard_map/psum | solution.py:257
  461.5 5.4 multiply_reduce_fusion.1
  473.4 7.2 fusion.20
  480.6 15.1 %copy.136 = f32[16,512,3,64]{3,2,1,0:T(4,128)} copy(f32[16,512,3,64]{1,3,2,0:T(8,128)} %fusion.20) | data formatting | bytes 12582912 | tf_op jit(solution)/shard_map/reshape | solution.py:132
  495.7 18.9 %reshape.553 = f32[128,64,192]{2,1,0:T(8,128)} reshape(f32[16,512,3,64]{3,2,1,0:T(4,128)} %copy.136) | data formatting | bytes 12582912 | tf_op jit(solution)/shard_map/reshape | solution.py:132
  517.0 26.2 %scatter_fusion.1 = f32[64,64,192]{2,1,0:T(8,128)} fusion(f32[64,64,192]{2,1,0:T(8,128)} %broadcast.358.clone, s32[128]{0:T(128)S(1)} %reshape.508, f32[128,64,192]{2,1,0:T(8,128)} %reshape.553), kind=kCustom, calls=%fused_computation.3 | custom fusion | flops 1572864 | bytes 18874880 | tf_op jit(solution)/shard_map/scatter-add | solution.py:132
  548.7 6.7 multiply_reduce_fusion
  564.5 15.1 %copy.135 = f32[16,512,3,64]{3,2,1,0:T(4,128)} copy(f32[16,512,3,64]{1,3,2,0:T(8,128)} %multiply_bitcast_fusion) | data formatting | bytes 12582912 | tf_op jit(solution)/shard_map/reshape | solution.py:127
  579.6 18.9 %reshape.552 = f32[128,64,192]{2,1,0:T(8,128)} reshape(f32[16,512,3,64]{3,2,1,0:T(4,128)} %copy.135) | data formatting | bytes 12582912 | tf_op jit(solution)/shard_map/reshape | solution.py:127
  601.0 26.2 %scatter_fusion = f32[64,64,192]{2,1,0:T(8,128)} fusion(f32[64,64,192]{2,1,0:T(8,128)} %broadcast.358.clone.1, s32[128]{0:T(128)S(1)} %reshape.508, f32[128,64,192]{2,1,0:T(8,128)} %reshape.552), kind=kCustom, calls=%fused_computation.2 | custom fusion | flops 1572864 | bytes 18874880 | tf_op jit(solution)/shard_map/scatter-add | solution.py:127
  681.3 7.7 pad_maximum_fusion
  689.7 19.4 %pmax.7 = f32[3]{0:T(128)S(1)} all-reduce(f32[3]{0:T(128)S(1)} %broadcast_maximum_fusion), channel_id=1, replica_groups=mesh['shard'=2,'ctx'=4,'tp'=4] {'shard','ctx'}, use_global_device_ids=true, to_apply=%region_32.33 | all-reduce | flops 3 | bytes 24 | tf_op jit(solution)/shard_map/pmax | solution.py:239
  710.0 22.3 %reduce-scatter.16.cloned.1.call-done = f32[96,6]{1,0:T(8,128)} async-done(((f32[768,6]{1,0:T(8,128)}), f32[96,6]{1,0:T(8,128)}) %reduce-scatter.16.cloned.1.call-update) | async-done | bytes 2320
  734.6 63.3 %reduce-scatter.18.cloned.1.call-done = f32[144,1]{1,0:T(8,128)} async-done(((f32[1152,1]{1,0:T(8,128)}), f32[144,1]{1,0:T(8,128)}) %reduce-scatter.18.cloned.1.call-update) | async-done | bytes 592
  800.1 42.6 %all-reduce.13.cloned.1.call-done = bf16[1024,768]{1,0:T(8,128)(2,1)} async-done(((bf16[1024,768]{1,0:T(8,128)(2,1)}), bf16[1024,768]{1,0:T(8,128)(2,1)}) %all-reduce.13.cloned.1.call-update) | async-done | bytes 1572880 | tf_op jit(solution)/shard_map/psum | solution.py:302
  846.7 162.3 %reduce-scatter.14.cloned.1.call-done = f32[24,96,96]{2,1,0:T(8,128)} async-done(((f32[192,96,96]{2,1,0:T(8,128)}), f32[24,96,96]{2,1,0:T(8,128)}) %reduce-scatter.14.cloned.1.call-update) | async-done | bytes 884752 | tf_op jit(solution)/shard_map/reduce_scatter | solution.py:312
  (325 shorter events, 199.4 us)
Async XLA Ops:
  7.2 1001.7 %copy-start = (f32[24,96,96]{2,1,0:T(8,128)S(1)}, f32[24,96,96]{2,1,0:T(8,128)}, u32[]{:S(2)}) copy-start(f32[24,96,96]{2,1,0:T(8,128)} %param.21) | copy-start | bytes 2654212
  7.2 85.6 %all-gather.6.cloned.1.call-start = ((), (), s32[]{:S(2)}) async-start(), calls=%async_computation.5 | async-start | bytes 5308416 | tf_op jit(solution)/shard_map/all_gather | solution.py:165
  9.5 127.0 %all-gather.10.cloned.1.call-start = ((), (), s32[]{:S(2)}) async-start(), calls=%async_computation.14 | async-start | bytes 1966080 | tf_op jit(solution)/shard_map/all_gather | solution.py:187
  101.0 73.7 %all-gather.8.cloned.1.call-start = ((), (), s32[]{:S(2)}) async-start(), calls=%async_computation.13 | async-start | bytes 1966080 | tf_op jit(solution)/shard_map/all_gather | solution.py:188
  103.4 186.4 %all-reduce.7.cloned.1.call-start = ((), (), s32[]{:S(2)}) async-start(), calls=%async_computation.6 | async-start | bytes 6291456 | tf_op jit(solution)/shard_map/psum | solution.py:225
  222.3 147.8 %all-reduce.9.cloned.1.call-start = ((), (), s32[]{:S(2)}) async-start(), calls=%async_computation.7 | async-start | bytes 6291456 | tf_op jit(solution)/shard_map/psum | solution.py:234
  223.9 68.9 %copy-start.43 = (f32[768]{0:T(1024)}, f32[768]{0:T(1024)S(1)}, u32[]{:S(2)}) copy-start(f32[768]{0:T(1024)S(1)} %get-tuple-element.22) | copy-start | bytes 9220
  223.9 68.9 %copy-start.49 = (f32[768]{0:T(1024)}, f32[768]{0:T(1024)S(1)}, u32[]{:S(2)}) copy-start(f32[768]{0:T(1024)S(1)} %get-tuple-element.21) | copy-start | bytes 9220
  233.3 56.5 %copy-start.23 = (bf16[1,1024,768]{2,1,0:T(8,128)(2,1)S(1)}, bf16[1,1024,768]{2,1,0:T(8,128)(2,1)}, u32[]{:S(2)}) copy-start(bf16[1,1024,768]{2,1,0:T(8,128)(2,1)} %param.12) | copy-start | bytes 4718596
  301.5 160.0 %all-reduce.11.cloned.1.call-start = ((), (), s32[]{:S(2)}) async-start(), calls=%async_computation.8 | async-start | bytes 6291456 | tf_op jit(solution)/shard_map/psum | solution.py:257
  392.8 68.7 %copy-start.42 = (f32[1024]{0:T(1024)S(1)}, f32[1024]{0:T(1024)}, u32[]{:S(2)}) copy-start(f32[1024]{0:T(1024)} %copy-done.41) | copy-start | bytes 12292
  392.8 68.7 %copy-start.44 = (f32[768]{0:T(1024)S(1)}, f32[768]{0:T(1024)}, u32[]{:S(2)}) copy-start(f32[768]{0:T(1024)} %copy-done.43) | copy-start | bytes 9220
  392.8 68.7 %copy-start.46 = (f32[1024]{0:T(1024)S(1)}, f32[1024]{0:T(1024)}, u32[]{:S(2)}) copy-start(f32[1024]{0:T(1024)} %copy-done.45) | copy-start | bytes 12292
  392.8 269.5 %reduce-scatter.12.cloned.1.call-start = ((), (), s32[]{:S(2)}) async-start(), calls=%async_computation.10 | async-start | bytes 1966080 | tf_op jit(solution)/shard_map/reduce_scatter | solution.py:291
  393.6 73.3 %copy-start.51 = (f32[1024]{0:T(1024)S(1)}, f32[1024]{0:T(1024)}, u32[]{:S(2)}) copy-start(f32[1024]{0:T(1024)} %copy-done.50) | copy-start | bytes 12292
  548.4 119.6 %reduce-scatter.10.cloned.1.call-start = ((), (), s32[]{:S(2)}) async-start(), calls=%async_computation.9 | async-start | bytes 1966080 | tf_op jit(solution)/shard_map/reduce_scatter | solution.py:288
  632.4 99.9 %reduce-scatter.16.cloned.1.call-start = ((), (), s32[]{:S(2)}) async-start(), calls=%async_computation.15 | async-start | bytes 442368
  662.2 135.6 %reduce-scatter.18.cloned.1.call-start = ((), (), s32[]{:S(2)}) async-start(), calls=%async_computation.16 | async-start | bytes 663552
  664.6 178.1 %all-reduce.13.cloned.1.call-start = ((), (), s32[]{:S(2)}) async-start(), calls=%async_computation.11 | async-start | bytes 3145728 | tf_op jit(solution)/shard_map/psum | solution.py:302
  672.1 336.8 %reduce-scatter.14.cloned.1.call-start = ((), (), s32[]{:S(2)}) async-start(), calls=%async_computation.12 | async-start | bytes 10616832 | tf_op jit(solution)/shard_map/reduce_scatter | solution.py:312
  733.2 109.5 %copy-start.58 = (f32[6,96]{1,0:T(8,128)}, f32[6,96]{1,0:T(8,128)S(1)}, u32[]{:S(2)}) copy-start(f32[6,96]{1,0:T(8,128)S(1)} %copy.138) | copy-start | bytes 6916
  798.8 43.9 %copy-start.66 = (f32[1,144]{1,0:T(1,128)}, f32[1,144]{1,0:T(1,128)S(1)}, u32[]{:S(2)}) copy-start(f32[1,144]{1,0:T(1,128)S(1)} %copy.140) | copy-start | bytes 1732
  846.7 164.8 %copy-start.18 = (f32[24,96,96]{2,1,0:T(8,128)S(1)}, f32[24,96,96]{2,1,0:T(8,128)}, u32[]{:S(2)}) copy-start(f32[24,96,96]{2,1,0:T(8,128)} %param.16) | copy-start | bytes 2654212
  846.7 164.8 %copy-start.27 = (f32[24,96,96]{2,1,0:T(8,128)S(1)}, f32[24,96,96]{2,1,0:T(8,128)}, u32[]{:S(2)}) copy-start(f32[24,96,96]{2,1,0:T(8,128)} %param.22) | copy-start | bytes 2654212
  (69 other events, 245.1 us)
Sparse Core Ops, SparseCore 0:
  10.7 82.0 all-gather.5
  101.1 35.3 all-gather.9
  138.7 35.9 all-gather.7
  222.5 67.2 all-reduce.6
  301.6 68.5 all-reduce.8
  392.9 68.5 all-reduce.10
  548.5 35.4 reduce-scatter.11
  632.5 35.4 reduce-scatter.9
  671.3 61.0 reduce-scatter.15
  736.0 61.7 reduce-scatter.17
  800.8 41.8 all-reduce.12
  846.7 162.1 reduce-scatter.13
where the time goes:
time: 1030 us
  waiting for transfers between devices  597 us (58%)
  local copies, waits for them, and re-layouts  215 us (21%)
  other arithmetic  108 us (10%)
  matrix products  69.6 us (7%)
  blocking collectives  19.4 us (2%)
  between operations  16.1 us (2%)
    reduce_scatter x1, waiting for transfers between devices, per_device(): lax.psum_scatter(blocks_grad, ('shard', 'ctx'), scatter_dimension=0, tile...  162 us
    unnamed x14, waiting for transfers between devices  85.7 us
    all_gather x1, waiting for transfers between devices, per_device(): lax.all_gather(master_blocks.astype(jnp.bfloat16), ('shard', 'ctx'), axis...  83.2 us
    psum x1, waiting for transfers between devices, per_device(): lax.psum(jnp.dot(d_gate_low, wb_up.T, preferred_element_type=jnp.float32)...  67.9 us
    psum x1, waiting for transfers between devices, per_device(): lax.psum(jnp.dot(act_low, w_down, preferred_element_type=jnp.float32), 'tp')  67.8 us
    reshape x4, local copies, waits for them, and re-layouts, pick_blocks(): picked.reshape(clipped.shape[0], clipped.shape[1] * BLOCK, head_count, HEAD)  56.3 us
    psum x1, waiting for transfers between devices, per_device(): lax.psum(jnp.dot(attended_low, w_out, preferred_element_type=jnp.float32)...  52.6 us
    psum x1, waiting for transfers between devices, per_device(): lax.psum(jnp.dot(d_proj, wb_qkv.T, preferred_element_type=jnp.float32).as...  42.6 us
  transfers between devices with their start and end apart: 12, of which 11 were waited for; matrix products, arithmetic and copies ran while one was open for 19% of the time, Pallas kernels for 0%

commit v1 on v0

--- a/solution.py
+++ b/solution.py
@@ -231,7 +231,10 @@
     gate_pre = jnp.dot(x_first_low, w_up, preferred_element_type=jnp.float32) + up_bias
     act_low = gelu_tanh(gate_pre).astype(jnp.bfloat16)
     ff_out = (
-        lax.psum(jnp.dot(act_low, w_down, preferred_element_type=jnp.float32), "tp")
+        jnp.sum(
+            lax.all_gather(jnp.dot(act_low, w_down, preferred_element_type=jnp.float32), "tp"),
+            axis=0,
+        )
         + outer_vectors[1]
     )
     mixed_sum = x_first + ff_out

time: 1030 us -> 1060 us (1.029)
  waiting for transfers between devices: 597 us -> 611 us
    all_gather x0 -> x1, waiting for transfers between devices: none -> 81.4 us  [per_device(): lax.all_gather(jnp.dot(act_low, w_down, preferred_element_type=jnp.float3...]
    psum x1 -> x0, waiting for transfers between devices: 67.8 us -> none  [per_device(): lax.psum(jnp.dot(act_low, w_down, preferred_element_type=jnp.float32), 'tp')]
where the time goes in v1:
time: 1060 us; the launch traced here: 1050 us
  waiting for transfers between devices  611 us (58%)
  local copies, waits for them, and re-layouts  215 us (20%)
  other arithmetic  116 us (11%)
  matrix products  69.6 us (7%)
  blocking collectives  19.5 us (2%)
  between operations  16.1 us (2%)
    reduce_scatter x1, waiting for transfers between devices, per_device(): lax.psum_scatter(blocks_grad, ('shard', 'ctx'), scatter_dimension=0, tile...  162 us
    unnamed x14, waiting for transfers between devices  85.7 us
    all_gather x1, waiting for transfers between devices, per_device(): lax.all_gather(master_blocks.astype(jnp.bfloat16), ('shard', 'ctx'), axis...  83.2 us
    all_gather x1, waiting for transfers between devices, per_device(): lax.all_gather(jnp.dot(act_low, w_down, preferred_element_type=jnp.float3...  81.4 us
    psum x1, waiting for transfers between devices, per_device(): lax.psum(jnp.dot(d_gate_low, wb_up.T, preferred_element_type=jnp.float32)...  67.8 us
    reshape x4, local copies, waits for them, and re-layouts, pick_blocks(): picked.reshape(clipped.shape[0], clipped.shape[1] * BLOCK, head_count, HEAD)  56.3 us
    psum x1, waiting for transfers between devices, per_device(): lax.psum(jnp.dot(attended_low, w_out, preferred_element_type=jnp.float32)...  52.6 us
    psum x1, waiting for transfers between devices, per_device(): lax.psum(jnp.dot(d_proj, wb_qkv.T, preferred_element_type=jnp.float32).as...  42.6 us
  transfers between devices with their start and end apart: 12, of which 11 were waited for; matrix products, arithmetic and copies ran while one was open for 19% of the time, Pallas kernels for 0%

profile of v1, /device:TPU:0, one launch (start us, length us, event | category | flops | bytes accessed | tf_op | source)
XLA Modules:
  0.0 1048.8 jit_solution(4084512842213533725)
XLA Ops:
  9.6 83.2 %all-gather.8.cloned.1.call-done = bf16[192,96,96]{2,1,0:T(8,128)(2,1)} async-done(((bf16[24,96,96]{2,1,0:T(8,128)(2,1)}), bf16[192,96,96]{2,1,0:T(8,128)(2,1)}) %all-gather.8.cloned.1.call-update) | async-done | bytes 3538960 | tf_op jit(solution)/shard_map/all_gather | solution.py:165
  109.1 27.4 %all-gather.12.cloned.1.call-done = bf16[4096,192]{0,1:T(8,128)(2,1)} async-done(((bf16[1024,192]{0,1:T(8,128)(2,1)}), bf16[4096,192]{0,1:T(8,128)(2,1)}) %all-gather.12.cloned.1.call-update) | async-done | bytes 1572880 | tf_op jit(solution)/shard_map/all_gather | solution.py:187
  142.4 15.9 %reshape.560 = bf16[16,512,3,64]{3,2,1,0:T(4,128)(2,1)} reshape(bf16[128,64,192]{2,1,0:T(8,128)(2,1)} %gather_fusion.1) | data formatting | bytes 6291456 | tf_op jit(solution)/shard_map/reshape | solution.py:73
  158.4 12.2 %copy.106 = bf16[16,512,3,64]{1,3,2,0:T(8,128)(2,1)} copy(bf16[16,512,3,64]{3,2,1,0:T(4,128)(2,1)} %reshape.560) | data formatting | bytes 6291456 | tf_op jit(solution)/shard_map/reshape | solution.py:73
  180.5 15.9 %reshape.559 = bf16[16,512,3,64]{3,2,1,0:T(4,128)(2,1)} reshape(bf16[128,64,192]{2,1,0:T(8,128)(2,1)} %gather_fusion) | data formatting | bytes 6291456 | tf_op jit(solution)/shard_map/reshape | solution.py:73
  196.4 12.3 %copy.107 = bf16[16,512,3,64]{1,3,2,0:T(8,128)(2,1)} copy(bf16[16,512,3,64]{3,2,1,0:T(4,128)(2,1)} %reshape.559) | data formatting | bytes 6291456 | tf_op jit(solution)/shard_map/reshape | solution.py:73
  237.2 52.6 %all-reduce.6.cloned.1.call-done = f32[1024,768]{1,0:T(8,128)} async-done(((f32[1024,768]{1,0:T(8,128)}), f32[1024,768]{1,0:T(8,128)}) %all-reduce.6.cloned.1.call-update) | async-done | bytes 3145744 | tf_op jit(solution)/shard_map/psum | solution.py:225
  302.4 81.4 %all-gather.14.cloned.1.call-done = f32[4096,768]{1,0:T(8,128)} async-done(((f32[1024,768]{1,0:T(8,128)}), f32[4096,768]{1,0:T(8,128)}) %all-gather.14.cloned.1.call-update) | async-done | bytes 12582928 | tf_op jit(solution)/shard_map/all_gather | solution.py:235
  383.8 7.4 reduce_sum.183
  414.7 67.8 %all-reduce.8.cloned.1.call-done = f32[1024,768]{1,0:T(8,128)} async-done(((f32[1024,768]{1,0:T(8,128)}), f32[1024,768]{1,0:T(8,128)}) %all-reduce.8.cloned.1.call-update) | async-done | bytes 3145744 | tf_op jit(solution)/shard_map/psum | solution.py:260
  494.4 7.2 fusion.20
  501.6 15.1 %copy.136 = f32[16,512,3,64]{3,2,1,0:T(4,128)} copy(f32[16,512,3,64]{1,3,2,0:T(8,128)} %fusion.20) | data formatting | bytes 12582912 | tf_op jit(solution)/shard_map/reshape | solution.py:132
  516.7 18.9 %reshape.554 = f32[128,64,192]{2,1,0:T(8,128)} reshape(f32[16,512,3,64]{3,2,1,0:T(4,128)} %copy.136) | data formatting | bytes 12582912 | tf_op jit(solution)/shard_map/reshape | solution.py:132
  538.0 26.2 %scatter_fusion.1 = f32[64,64,192]{2,1,0:T(8,128)} fusion(f32[64,64,192]{2,1,0:T(8,128)} %broadcast.358.clone, s32[128]{0:T(128)S(1)} %reshape.508, f32[128,64,192]{2,1,0:T(8,128)} %reshape.554), kind=kCustom, calls=%fused_computation.3 | custom fusion | flops 1572864 | bytes 18874880 | tf_op jit(solution)/shard_map/scatter-add | solution.py:132
  569.6 6.7 multiply_reduce_fusion
  585.5 15.1 %copy.135 = f32[16,512,3,64]{3,2,1,0:T(4,128)} copy(f32[16,512,3,64]{1,3,2,0:T(8,128)} %multiply_bitcast_fusion) | data formatting | bytes 12582912 | tf_op jit(solution)/shard_map/reshape | solution.py:127
  600.6 18.9 %reshape.553 = f32[128,64,192]{2,1,0:T(8,128)} reshape(f32[16,512,3,64]{3,2,1,0:T(4,128)} %copy.135) | data formatting | bytes 12582912 | tf_op jit(solution)/shard_map/reshape | solution.py:127
  622.0 26.2 %scatter_fusion = f32[64,64,192]{2,1,0:T(8,128)} fusion(f32[64,64,192]{2,1,0:T(8,128)} %broadcast.358.clone.1, s32[128]{0:T(128)S(1)} %reshape.508, f32[128,64,192]{2,1,0:T(8,128)} %reshape.553), kind=kCustom, calls=%fused_computation.2 | custom fusion | flops 1572864 | bytes 18874880 | tf_op jit(solution)/shard_map/scatter-add | solution.py:127
  702.3 7.7 pad_maximum_fusion
  710.6 19.5 %pmax.7 = f32[3]{0:T(128)S(1)} all-reduce(f32[3]{0:T(128)S(1)} %broadcast_maximum_fusion), channel_id=1, replica_groups=mesh['shard'=2,'ctx'=4,'tp'=4] {'shard','ctx'}, use_global_device_ids=true, to_apply=%region_32.33 | all-reduce | flops 3 | bytes 24 | tf_op jit(solution)/shard_map/pmax | solution.py:242
  731.1 22.3 %reduce-scatter.16.cloned.1.call-done = f32[96,6]{1,0:T(8,128)} async-done(((f32[768,6]{1,0:T(8,128)}), f32[96,6]{1,0:T(8,128)}) %reduce-scatter.16.cloned.1.call-update) | async-done | bytes 2320
  755.6 63.3 %reduce-scatter.18.cloned.1.call-done = f32[144,1]{1,0:T(8,128)} async-done(((f32[1152,1]{1,0:T(8,128)}), f32[144,1]{1,0:T(8,128)}) %reduce-scatter.18.cloned.1.call-update) | async-done | bytes 592
  821.1 42.6 %all-reduce.10.cloned.1.call-done = bf16[1024,768]{1,0:T(8,128)(2,1)} async-done(((bf16[1024,768]{1,0:T(8,128)(2,1)}), bf16[1024,768]{1,0:T(8,128)(2,1)}) %all-reduce.10.cloned.1.call-update) | async-done | bytes 1572880 | tf_op jit(solution)/shard_map/psum | solution.py:305
  867.7 162.3 %reduce-scatter.14.cloned.1.call-done = f32[24,96,96]{2,1,0:T(8,128)} async-done(((f32[192,96,96]{2,1,0:T(8,128)}), f32[24,96,96]{2,1,0:T(8,128)}) %reduce-scatter.14.cloned.1.call-update) | async-done | bytes 884752 | tf_op jit(solution)/shard_map/reduce_scatter | solution.py:315
  (326 shorter events, 204.7 us)
Async XLA Ops:
  7.2 1022.7 %copy-start = (f32[24,96,96]{2,1,0:T(8,128)S(1)}, f32[24,96,96]{2,1,0:T(8,128)}, u32[]{:S(2)}) copy-start(f32[24,96,96]{2,1,0:T(8,128)} %param.21) | copy-start | bytes 2654212
  7.2 85.6 %all-gather.8.cloned.1.call-start = ((), (), s32[]{:S(2)}) async-start(), calls=%async_computation.5 | async-start | bytes 5308416 | tf_op jit(solution)/shard_map/all_gather | solution.py:165
  9.5 127.0 %all-gather.12.cloned.1.call-start = ((), (), s32[]{:S(2)}) async-start(), calls=%async_computation.13 | async-start | bytes 1966080 | tf_op jit(solution)/shard_map/all_gather | solution.py:187
  101.0 73.7 %all-gather.10.cloned.1.call-start = ((), (), s32[]{:S(2)}) async-start(), calls=%async_computation.12 | async-start | bytes 1966080 | tf_op jit(solution)/shard_map/all_gather | solution.py:188
  103.4 186.4 %all-reduce.6.cloned.1.call-start = ((), (), s32[]{:S(2)}) async-start(), calls=%async_computation.6 | async-start | bytes 6291456 | tf_op jit(solution)/shard_map/psum | solution.py:225
  222.3 161.5 %all-gather.14.cloned.1.call-start = ((), (), s32[]{:S(2)}) async-start(), calls=%async_computation.14 | async-start | bytes 15728640 | tf_op jit(solution)/shard_map/all_gather | solution.py:235
  223.9 68.9 %copy-start.43 = (f32[768]{0:T(1024)}, f32[768]{0:T(1024)S(1)}, u32[]{:S(2)}) copy-start(f32[768]{0:T(1024)S(1)} %get-tuple-element.22) | copy-start | bytes 9220
  223.9 68.9 %copy-start.49 = (f32[768]{0:T(1024)}, f32[768]{0:T(1024)S(1)}, u32[]{:S(2)}) copy-start(f32[768]{0:T(1024)S(1)} %get-tuple-element.21) | copy-start | bytes 9220
  233.3 56.5 %copy-start.23 = (bf16[1,1024,768]{2,1,0:T(8,128)(2,1)S(1)}, bf16[1,1024,768]{2,1,0:T(8,128)(2,1)}, u32[]{:S(2)}) copy-start(bf16[1,1024,768]{2,1,0:T(8,128)(2,1)} %param.12) | copy-start | bytes 4718596
  301.5 181.0 %all-reduce.8.cloned.1.call-start = ((), (), s32[]{:S(2)}) async-start(), calls=%async_computation.7 | async-start | bytes 6291456 | tf_op jit(solution)/shard_map/psum | solution.py:260
  413.9 68.7 %copy-start.42 = (f32[1024]{0:T(1024)S(1)}, f32[1024]{0:T(1024)}, u32[]{:S(2)}) copy-start(f32[1024]{0:T(1024)} %copy-done.41) | copy-start | bytes 12292
  413.9 68.7 %copy-start.44 = (f32[768]{0:T(1024)S(1)}, f32[768]{0:T(1024)}, u32[]{:S(2)}) copy-start(f32[768]{0:T(1024)} %copy-done.43) | copy-start | bytes 9220
  413.9 68.6 %copy-start.46 = (f32[1024]{0:T(1024)S(1)}, f32[1024]{0:T(1024)}, u32[]{:S(2)}) copy-start(f32[1024]{0:T(1024)} %copy-done.45) | copy-start | bytes 12292
  413.9 269.4 %reduce-scatter.12.cloned.1.call-start = ((), (), s32[]{:S(2)}) async-start(), calls=%async_computation.9 | async-start | bytes 1966080 | tf_op jit(solution)/shard_map/reduce_scatter | solution.py:294
  414.6 73.2 %copy-start.51 = (f32[1024]{0:T(1024)S(1)}, f32[1024]{0:T(1024)}, u32[]{:S(2)}) copy-start(f32[1024]{0:T(1024)} %copy-done.50) | copy-start | bytes 12292
  569.4 119.6 %reduce-scatter.10.cloned.1.call-start = ((), (), s32[]{:S(2)}) async-start(), calls=%async_computation.8 | async-start | bytes 1966080 | tf_op jit(solution)/shard_map/reduce_scatter | solution.py:291
  653.4 99.9 %reduce-scatter.16.cloned.1.call-start = ((), (), s32[]{:S(2)}) async-start(), calls=%async_computation.15 | async-start | bytes 442368
  683.2 135.6 %reduce-scatter.18.cloned.1.call-start = ((), (), s32[]{:S(2)}) async-start(), calls=%async_computation.16 | async-start | bytes 663552
  685.6 178.2 %all-reduce.10.cloned.1.call-start = ((), (), s32[]{:S(2)}) async-start(), calls=%async_computation.10 | async-start | bytes 3145728 | tf_op jit(solution)/shard_map/psum | solution.py:305
  693.1 336.8 %reduce-scatter.14.cloned.1.call-start = ((), (), s32[]{:S(2)}) async-start(), calls=%async_computation.11 | async-start | bytes 10616832 | tf_op jit(solution)/shard_map/reduce_scatter | solution.py:315
  754.2 109.6 %copy-start.58 = (f32[6,96]{1,0:T(8,128)}, f32[6,96]{1,0:T(8,128)S(1)}, u32[]{:S(2)}) copy-start(f32[6,96]{1,0:T(8,128)S(1)} %copy.138) | copy-start | bytes 6916
  819.8 43.9 %copy-start.66 = (f32[1,144]{1,0:T(1,128)}, f32[1,144]{1,0:T(1,128)S(1)}, u32[]{:S(2)}) copy-start(f32[1,144]{1,0:T(1,128)S(1)} %copy.140) | copy-start | bytes 1732
  867.7 164.8 %copy-start.18 = (f32[24,96,96]{2,1,0:T(8,128)S(1)}, f32[24,96,96]{2,1,0:T(8,128)}, u32[]{:S(2)}) copy-start(f32[24,96,96]{2,1,0:T(8,128)} %param.16) | copy-start | bytes 2654212
  867.7 164.8 %copy-start.27 = (f32[24,96,96]{2,1,0:T(8,128)S(1)}, f32[24,96,96]{2,1,0:T(8,128)}, u32[]{:S(2)}) copy-start(f32[24,96,96]{2,1,0:T(8,128)} %param.22) | copy-start | bytes 2654212
  (69 other events, 245.1 us)
Sparse Core Ops, SparseCore 0:
  10.7 82.0 all-gather.7
  101.1 35.3 all-gather.11
  138.7 35.9 all-gather.9
  222.5 67.2 all-reduce.5
  301.6 82.1 all-gather.13
  414.0 68.4 all-reduce.7
  569.5 35.4 reduce-scatter.11
  653.5 35.4 reduce-scatter.9
  692.2 61.0 reduce-scatter.15
  757.0 61.7 reduce-scatter.17
  821.8 41.8 all-reduce.9
  867.7 162.1 reduce-scatter.13
